TPU v7x, 32 devices: a whole 2x2x4 slice. The times are simulated.
32 devices in a mesh: gx: 4 (over y, core), gy: 8 (over z, x).
Axes of the slice: x: 2, y: 2, z: 4, core: 2. Of those that a mesh axis runs over, the one named last changes fastest.
Arguments:
- hidden: bfloat16 [128, 64, 4096], P(('gx', 'gy')), may hold values from -6 to 6
- parents: int32 [128, 64], P(('gx', 'gy')), may hold values from -1 to 62, as said below
- accepted: int32 [128, 64], P(('gx', 'gy')), may hold values 0 or 1
- token_ids: int32 [128, 64], P(('gx', 'gy')), may hold values from 0 to 128255
Outputs:
- dest_rows: bfloat16 [1024, 4096], P(('gx', 'gy'))
- accept_len: int32 [128], P(('gx', 'gy'))
- offsets: int32 [128], P(('gx', 'gy'))
- next_token: int32 [128], P(('gx', 'gy'))
Inputs may be any that keep to these rules, and one draw needn't show every extreme that they name: parents[r, n] < n; node 0 is the only root; nodes 1 to 7 each have the previous node as parent; every node has depth at most 7.
All inputs are finite; a program needn't handle non-finite values. No bound on the sum of `accepted` on one device may be relied on, other than what follows from the above.
Results may differ from a plain program's by a relative error of at most 0.001.
Values may be sent and summed in bfloat16 or wider, within the bound.
A program may use at most 64 MiB of HBM per device.

v0:
```python
import jax
import jax.numpy as jnp
from jax import lax
from jax.sharding import PartitionSpec as P

DEPTH = 8


def pick_from(table, hot):
    return jnp.sum(jnp.where(hot, table, 0), axis=-1)


def tree_walk(parents, accepted):
    nodes = parents.shape[1]
    index = jnp.arange(nodes, dtype=jnp.int32)[None, :]
    is_root = parents < 0
    parent_hot = parents[:, :, None] == jnp.arange(nodes, dtype=jnp.int32)[None, None, :]
    depth = jnp.zeros(parents.shape, jnp.int32)
    alive = jnp.ones(parents.shape, jnp.int32)
    for step in range(DEPTH):
        depth_up = pick_from(depth[:, None, :], parent_hot)
        alive_up = pick_from(alive[:, None, :], parent_hot)
        depth = jnp.where(is_root, 0, depth_up + 1)
        alive = jnp.where(is_root, 1, accepted * alive_up)
    score = jnp.where(alive == 1, depth * nodes + (nodes - 1 - index), -1)
    best = jnp.argmax(score, axis=1)
    best_hot = index == best[:, None]
    length = pick_from(depth, best_hot) + 1
    on_path = jnp.zeros(parents.shape, jnp.bool_)
    current = best
    for step in range(DEPTH):
        current_hot = (index == current[:, None]) & (current[:, None] >= 0)
        on_path = on_path | current_hot
        upward = pick_from(parents, current_hot)
        current = jnp.where(current >= 0, upward, -1)
    return (depth, on_path, best_hot, length)


def local(hidden, parents, accepted, token_ids):
    requests, nodes, width = hidden.shape
    block = requests * DEPTH
    devices = lax.axis_size(("gx", "gy"))
    position = lax.axis_index(("gx", "gy"))
    depth, on_path, best_hot, length = tree_walk(parents, accepted)
    local_start = jnp.cumsum(length) - length
    count = jnp.sum(length)
    every_count = lax.all_gather(count[None], ("gx", "gy"), axis=0, tiled=True)
    lower = jnp.arange(devices, dtype=jnp.int32) < position
    before = jnp.sum(jnp.where(lower, every_count, 0))
    next_token = pick_from(token_ids, best_hot)
    node_rank = (local_start[:, None] + depth).reshape(1, -1)
    peers = jnp.arange(devices, dtype=jnp.int32)
    peer_rank = jnp.mod(peers - before, devices)
    valid = peer_rank < count
    table = ((peer_rank[:, None] == node_rank) & on_path.reshape(1, -1) & valid[:, None]).astype(
        jnp.bfloat16
    )
    outgoing = jnp.dot(
        table, hidden.reshape(requests * nodes, width), preferred_element_type=jnp.float32
    ).astype(jnp.bfloat16)
    slot_tag = jnp.where(valid, (before + peer_rank) // devices + 1, 0).astype(jnp.bfloat16)
    rows_in, tags_in = (
        lax.all_to_all(outgoing, ("gx", "gy"), split_axis=0, concat_axis=0, tiled=True),
        lax.all_to_all(slot_tag, ("gx", "gy"), split_axis=0, concat_axis=0, tiled=True),
    )
    slots = jnp.arange(block, dtype=jnp.int32)[:, None]
    placing = (slots == (tags_in.astype(jnp.int32) - 1)[None, :]).astype(jnp.bfloat16)
    dest_rows = jnp.dot(placing, rows_in, preferred_element_type=jnp.float32).astype(jnp.bfloat16)
    return (dest_rows, length, local_start + before, next_token)


def solution(mesh):
    placed = (
        P(("gx", "gy"), None, None),
        P(("gx", "gy"), None),
        P(("gx", "gy"), None),
        P(("gx", "gy"), None),
    )
    return jax.shard_map(
        local,
        mesh=mesh,
        in_specs=placed,
        out_specs=(P(("gx", "gy"), None), P(("gx", "gy")), P(("gx", "gy")), P(("gx", "gy"))),
        check_vma=False,
    )
```

profile of v0, /device:TPU:0, one launch (start us, length us, event | category | flops | bytes accessed | tf_op | source)
XLA Modules:
  0.0 95.9 jit_solution(2117214062581812011)
XLA Ops:
  0.6 0.0 copy-start
  0.7 1.0 %select_reduce_fusion.14 = s32[4,64]{1,0:T(4,128)S(1)} fusion(s32[4,64]{1,0:T(4,128)} %param.5), kind=kLoop, calls=%fused_computation.19 | loop fusion | flops 48896 | bytes 2048 | tf_op jit(solution)/shard_map/reduce_sum | solution.py:10
  1.7 0.7 multiply_select_fusion.6
  2.4 1.0 %select_reduce_fusion.6 = (s32[4,64]{1,0:T(4,128)S(1)}, s32[4,64]{1,0:T(4,128)S(1)}) fusion(s32[4,64]{1,0:T(4,128)S(1)} %broadcast_select_fusion, s32[4,64]{1,0:T(4,128)} %param.5, s32[4,64]{1,0:T(4,128)S(1)} %get-tuple-element.41), kind=kLoop, calls=%fused_computation.11 | loop fusion | flops 81408 | bytes 5120 | tf_op jit(solution)/shard_map/reduce_sum | solution.py:10
  3.4 0.7 multiply_select_fusion.5
  4.1 1.0 %select_reduce_fusion.5 = (s32[4,64]{1,0:T(4,128)S(1)}, s32[4,64]{1,0:T(4,128)S(1)}) fusion(s32[4,64]{1,0:T(4,128)S(1)} %get-tuple-element.54, s32[4,64]{1,0:T(4,128)} %param.5, s32[4,64]{1,0:T(4,128)S(1)} %get-tuple-element.53), kind=kLoop, calls=%fused_computation.10 | loop fusion | flops 81408 | bytes 5120 | tf_op jit(solution)/shard_map/reduce_sum | solution.py:10
  5.1 0.7 multiply_select_fusion.4
  5.8 1.0 %select_reduce_fusion.4 = (s32[4,64]{1,0:T(4,128)S(1)}, s32[4,64]{1,0:T(4,128)S(1)}) fusion(s32[4,64]{1,0:T(4,128)S(1)} %get-tuple-element.52, s32[4,64]{1,0:T(4,128)} %param.5, s32[4,64]{1,0:T(4,128)S(1)} %get-tuple-element.51), kind=kLoop, calls=%fused_computation.9 | loop fusion | flops 81408 | bytes 5120 | tf_op jit(solution)/shard_map/reduce_sum | solution.py:10
  6.8 0.7 multiply_select_fusion.3
  7.5 1.0 %select_reduce_fusion.3 = (s32[4,64]{1,0:T(4,128)S(1)}, s32[4,64]{1,0:T(4,128)S(1)}) fusion(s32[4,64]{1,0:T(4,128)S(1)} %get-tuple-element.50, s32[4,64]{1,0:T(4,128)} %param.5, s32[4,64]{1,0:T(4,128)S(1)} %get-tuple-element.49), kind=kLoop, calls=%fused_computation.8 | loop fusion | flops 81408 | bytes 5120 | tf_op jit(solution)/shard_map/reduce_sum | solution.py:10
  8.4 0.7 multiply_select_fusion.2
  9.1 1.0 %select_reduce_fusion.2 = (s32[4,64]{1,0:T(4,128)S(1)}, s32[4,64]{1,0:T(4,128)S(1)}) fusion(s32[4,64]{1,0:T(4,128)S(1)} %get-tuple-element.48, s32[4,64]{1,0:T(4,128)} %param.5, s32[4,64]{1,0:T(4,128)S(1)} %get-tuple-element.47), kind=kLoop, calls=%fused_computation.7 | loop fusion | flops 81408 | bytes 5120 | tf_op jit(solution)/shard_map/reduce_sum | solution.py:10
  10.1 0.7 multiply_select_fusion.1
  10.8 1.0 %select_reduce_fusion.1 = (s32[4,64]{1,0:T(4,128)S(1)}, s32[4,64]{1,0:T(4,128)S(1)}) fusion(s32[4,64]{1,0:T(4,128)S(1)} %get-tuple-element.46, s32[4,64]{1,0:T(4,128)} %param.5, s32[4,64]{1,0:T(4,128)S(1)} %get-tuple-element.45), kind=kLoop, calls=%fused_computation.6 | loop fusion | flops 81408 | bytes 5120 | tf_op jit(solution)/shard_map/reduce_sum | solution.py:10
  11.8 0.7 multiply_select_fusion
  12.5 1.0 %select_reduce_fusion = (s32[4,64]{1,0:T(4,128)S(1)}, s32[4,64]{1,0:T(4,128)S(1)}) fusion(s32[4,64]{1,0:T(4,128)S(1)} %get-tuple-element.44, s32[4,64]{1,0:T(4,128)} %param.5, s32[4,64]{1,0:T(4,128)S(1)} %get-tuple-element.43), kind=kLoop, calls=%fused_computation.5 | loop fusion | flops 81408 | bytes 5120 | tf_op jit(solution)/shard_map/reduce_sum | solution.py:10
  13.4 1.3 %iota_reduce_fusion = (s32[4]{0:T(128)}, s32[4]{0:T(128)S(1)}) fusion(pred[4,64]{1,0:T(4,128)(4,1)S(1)} %get-tuple-element.42, s32[4,64]{1,0:T(4,128)} %param.6, s32[4,64]{1,0:T(4,128)S(1)} %get-tuple-element.7, s32[64]{0:T(128)S(1)} %iota_subtract_fusion, s32[4,64]{1,0:T(4,128)S(1)} %get-tuple-element.6), kind=kLoop, calls=%fused_computation.59 | loop fusion | flops 3812 | bytes 3616 | tf_op jit(solution)/shard_map/tree_walk/reduce | solution.py:26
  14.8 1.4 %select_reduce_fusion.15 = (s32[4]{0:T(128)}, s32[4]{0:T(128)S(1)}, s32[4]{0:T(128)S(1)}) fusion(s32[4,64]{1,0:T(4,128)} %param.7, s32[4]{0:T(128)S(1)} %get-tuple-element.5, s32[4,64]{1,0:T(4,128)} %param.5, pred[4]{0:T(512)(128)(4,1)S(1)} %broadcast_compare_fusion.9, pred[4,64]{1,0:T(4,128)(4,1)S(1)} %get-tuple-element.42, s32[4,64]{1,0:T(4,128)S(1)} %get-tuple-element.6), kind=kLoop, calls=%fused_computation.43 | loop fusion | flops 2548 | bytes 3396 | tf_op jit(solution)/shard_map/reduce_sum | solution.py:10
  16.2 0.6 fusion.24
  16.8 0.0 copy-start.1
  16.8 0.8 dynamic-update-slice
  17.6 41.9 %all-reduce = s32[32]{0:T(128)S(1)} all-reduce(s32[32]{0:T(128)S(1)} %dynamic-update-slice), channel_id=1, replica_groups=mesh['gx'=4,'gy'=8] {'gx','gy'}, use_global_device_ids=true, to_apply=%add | all-reduce | flops 32 | bytes 256
  59.5 0.6 fusion.22
  60.1 2.0 %fusion.6 = bf16[32,1,1]{2,1,0:T(2,128)(2,1)} fusion(s32[]{:T(128)} %get-tuple-element.39, s32[]{:T(128)} %fusion.22), kind=kLoop, calls=%fused_computation.32 | loop fusion | flops 1024 | bytes 72 | tf_op jit(solution)/shard_map/convert_element_type | solution.py:61
  62.2 4.4 %all-to-all-start = ((bf16[32,1,1]{2,1,0:T(2,128)(2,1)}), bf16[32,1,1]{2,1,0:T(2,128)(2,1)S(1)}, u32[]{:S(2)}, u32[]{:S(2)}) async-start(bf16[32,1,1]{2,1,0:T(2,128)(2,1)} %fusion.6), calls=%async_computation | async-start | bytes 32768 | tf_op jit(solution)/shard_map/all_to_all | solution.py:64
  66.6 1.3 %broadcast_compare_fusion.1 = pred[32]{0:T(512)(128)(4,1)S(1)} fusion(s32[]{:T(128)} %get-tuple-element.39, s32[]{:T(128)} %fusion.22), kind=kLoop, calls=%fused_computation.95 | loop fusion | flops 416 | bytes 40 | tf_op jit(solution)/shard_map/lt | solution.py:54
  67.9 0.7 and_select_fusion.2
  68.6 0.9 select_reduce_fusion.21
  69.4 0.9 select_reduce_fusion.20
  70.3 0.9 select_reduce_fusion.19
  71.2 0.9 select_reduce_fusion.18
  72.1 0.9 select_reduce_fusion.17
  73.0 0.9 select_reduce_fusion.16
  73.8 0.1 fusion.21
  73.9 0.1 reshape.406
  74.0 0.2 reduce-window.7
  74.2 1.2 %broadcast_add_fusion.1 = (s32[4]{0:T(128)}, s32[4]{0:T(128)S(1)}) fusion(s32[]{:T(128)} %fusion.22, s32[4]{0:T(128)S(1)} %get-tuple-element.40, s32[4,1]{0,1:T(1,128)S(1)} %reduce-window.7), kind=kLoop, calls=%fused_computation.94 | loop fusion | flops 8 | bytes 68 | tf_op jit(solution)/shard_map/add | solution.py:69
  75.4 0.1 broadcast_add_fusion
  75.4 0.1 eq.210
  75.5 0.0 copy-done
  75.5 0.5 fusion
  76.0 0.5 broadcast.346
  76.5 0.8 reduce.21
  77.3 0.9 reshape.410
  78.2 0.0 all-to-all-done
  78.2 5.8 %all-to-all-start.1 = ((bf16[32,2,2048]{2,1,0:T(2,128)(2,1)}), bf16[32,2,2048]{2,1,0:T(2,128)(2,1)S(1)}, u32[]{:S(2)}, u32[]{:S(2)}) async-start(bf16[32,2,2048]{2,1,0:T(2,128)(2,1)} %reshape.410), calls=%async_computation.1 | async-start | bytes 524288 | tf_op jit(solution)/shard_map/all_to_all | solution.py:63
  84.0 0.7 add_reduce_fusion
  84.7 9.8 %all-to-all-done.1 = bf16[32,2,2048]{2,1,0:T(2,128)(2,1)S(1)} async-done(((bf16[32,2,2048]{2,1,0:T(2,128)(2,1)}), bf16[32,2,2048]{2,1,0:T(2,128)(2,1)S(1)}, u32[]{:S(2)}, u32[]{:S(2)}) %all-to-all-start.1) | async-done | bytes 262176 | tf_op jit(solution)/shard_map/all_to_all | solution.py:63
  94.5 0.3 reshape.411
  94.8 0.0 copy-done.1
  94.8 1.1 %convolution_convert_fusion = bf16[32,4096]{1,0:T(8,128)(2,1)} fusion(bf16[32,1,4096]{2,1,0:T(2,128)(2,1)S(1)} %reshape.411, s32[32]{0:T(128)S(1)} %add_reduce_fusion), kind=kOutput, calls=%fused_computation | convolution fusion | flops 8520704 | bytes 524416 | tf_op jit(solution)/shard_map/dot_general | solution.py:68
  (11 shorter events, 0.1 us)
Async XLA Ops:
  0.6 74.9 %copy-start = (bf16[4,64,4096]{2,1,0:T(8,128)(2,1)S(1)}, bf16[4,64,4096]{2,1,0:T(8,128)(2,1)}, u32[]{:S(2)}) copy-start(bf16[4,64,4096]{2,1,0:T(8,128)(2,1)} %param.4) | copy-start | bytes 6291460
  16.8 78.0 %copy-start.1 = (s32[4]{0:T(128)}, s32[4]{0:T(128)S(1)}, u32[]{:S(2)}) copy-start(s32[4]{0:T(128)S(1)} %get-tuple-element.40) | copy-start | bytes 52
  62.2 16.0 %all-to-all-start = ((bf16[32,1,1]{2,1,0:T(2,128)(2,1)}), bf16[32,1,1]{2,1,0:T(2,128)(2,1)S(1)}, u32[]{:S(2)}, u32[]{:S(2)}) async-start(bf16[32,1,1]{2,1,0:T(2,128)(2,1)} %fusion.6), calls=%async_computation | async-start | bytes 32768 | tf_op jit(solution)/shard_map/all_to_all | solution.py:64
  78.2 16.3 %all-to-all-start.1 = ((bf16[32,2,2048]{2,1,0:T(2,128)(2,1)}), bf16[32,2,2048]{2,1,0:T(2,128)(2,1)S(1)}, u32[]{:S(2)}, u32[]{:S(2)}) async-start(bf16[32,2,2048]{2,1,0:T(2,128)(2,1)} %reshape.410), calls=%async_computation.1 | async-start | bytes 524288 | tf_op jit(solution)/shard_map/all_to_all | solution.py:63
where the time goes:
time: 96.9 us; the launch traced here: 95.9 us
  blocking collectives  41.9 us (43%)
  other arithmetic  28.9 us (30%)
  starting transfers between devices  10.2 us (11%)
  waiting for transfers between devices  9.78 us (10%)
  local copies, waits for them, and re-layouts  2.62 us (3%)
  matrix products  1.62 us (2%)
    unnamed x1, blocking collectives  41.9 us
    reduce_sum x15, other arithmetic, pick_from(): return jnp.sum(jnp.where(hot, table, 0), axis=-1)  14.5 us
    all_to_all x1, waiting for transfers between devices, local(): lax.all_to_all(outgoing, ('gx', 'gy'), split_axis=0, concat_axis=0, tiled...  9.78 us
    all_to_all x1, starting transfers between devices, local(): lax.all_to_all(outgoing, ('gx', 'gy'), split_axis=0, concat_axis=0, tiled...  5.83 us
    select_n x7, other arithmetic, tree_walk(): alive = jnp.where(is_root, 1, accepted * alive_up)  4.87 us
    all_to_all x1, starting transfers between devices, local(): lax.all_to_all(slot_tag, ('gx', 'gy'), split_axis=0, concat_axis=0, tiled...  4.4 us
    convert_element_type x1, other arithmetic, local(): jnp.where(valid, (before + peer_rank) // devices + 1, 0)  2.04 us
  transfers between devices with their start and end apart: 2, of which 1 were waited for; matrix products, arithmetic and copies ran while one was open for 13% of the time, Pallas kernels for 0%

commit v1 on v0

v1 whole, which is shorter than its diff:
```python
import functools

import jax
import jax.numpy as jnp
from jax import lax
from jax.experimental import pallas as pl
from jax.experimental.pallas import tpu as pltpu
from jax.sharding import PartitionSpec as P

DEPTH = 8
FOLD = 16
MESH = pl.DeviceIdType.MESH


def mod(value, size):
    return value & (size - 1) if size & (size - 1) == 0 else lax.rem(value, size)


def div(value, size):
    if size & (size - 1) == 0:
        return lax.shift_right_logical(value, jnp.int32(size.bit_length() - 1) + jnp.zeros_like(value))
    return lax.div(value, jnp.int32(size) + jnp.zeros_like(value))


def lanes_of(table):
    return jnp.concatenate([table[r : r + 1, :] for r in range(table.shape[0])], axis=1)


def one_hot(rows, target):
    shape = (rows, target.shape[1])
    return (lax.broadcasted_iota(jnp.int32, shape, 0) == target).astype(jnp.bfloat16)


def kernel(
    sizes,
    hidden_ref,
    parents_ref,
    accepted_ref,
    tokens_ref,
    dest_ref,
    length_ref,
    offsets_ref,
    next_ref,
    hidden,
    staged,
    outgoing,
    incoming,
    count_out,
    counts,
    load_sem,
    own_sem,
    count_send,
    count_recv,
    row_send,
    row_recv,
):
    n_gx, n_gy, requests, nodes, width, block = sizes
    devices = n_gx * n_gy
    slab = width // FOLD
    every = requests * nodes
    me = lax.axis_index("gx") * n_gy + lax.axis_index("gy")

    def place(index):
        return (lax.div(index, n_gy), lax.rem(index, n_gy))

    def after(step):
        return lax.rem(me + step, devices)

    def ahead(step):
        return lax.rem(me + devices - step, devices)

    load = pltpu.make_async_copy(hidden_ref, hidden, load_sem)
    load.start()
    barrier = pltpu.get_barrier_semaphore()

    def greet(step, carry):
        pl.semaphore_signal(barrier, inc=1, device_id=place(after(step)), device_id_type=MESH)
        return carry

    lax.fori_loop(1, devices, greet, 0)

    lane = lax.broadcasted_iota(jnp.int32, (1, every), 1)
    group = div(lane, nodes)
    parents = lanes_of(parents_ref[...])
    bad = (parents >= 0) & (lanes_of(accepted_ref[...]) == 0)
    up = jnp.where(parents < 0, -1, parents + group * nodes)
    row = lax.broadcasted_iota(jnp.int32, (every, every), 0)
    col = lax.broadcasted_iota(jnp.int32, (every, every), 1)
    step_up = ((row == up) | (row == col)).astype(jnp.bfloat16)
    reach = step_up
    hops = 1
    while hops < DEPTH - 1:
        reach = jnp.dot(reach, reach, preferred_element_type=jnp.float32).astype(jnp.bfloat16)
        hops *= 2
    reach = (reach > 0).astype(jnp.bfloat16)
    which = lax.broadcasted_iota(jnp.int32, (16, every), 0)
    probe = jnp.where(which == 0, 1.0, jnp.where(bad, 1.0, 0.0)).astype(jnp.bfloat16)
    tally = jnp.dot(probe, reach, preferred_element_type=jnp.float32).astype(jnp.int32)
    depth = tally[0:1, :] - 1
    alive = tally[1:2, :] == 0
    score = jnp.where(alive, depth * nodes + (nodes - 1 - mod(lane, nodes)), -1)
    pad = 16
    mine = lax.broadcasted_iota(jnp.int32, (pad, every), 0) == group
    scores = jnp.where(mine, score, -1)
    top = jnp.max(scores.astype(jnp.float32), axis=1, keepdims=True).astype(jnp.int32)
    best_hot = mine & (scores == top)
    path = lax.dot_general(
        jnp.where(best_hot, 1.0, 0.0).astype(jnp.bfloat16),
        reach,
        (((1,), (1,)), ((), ())),
        preferred_element_type=jnp.float32,
    ).astype(jnp.int32)
    request = lax.broadcasted_iota(jnp.int32, (pad, 1), 0)
    length = jnp.where(request < requests, div(jnp.maximum(top, 0), nodes) + 1, 0)
    starts = []
    total = jnp.zeros((1, 1), jnp.int32)
    for r in range(requests):
        starts.append(total)
        total = total + length[r : r + 1, :]

    own_count = jnp.broadcast_to(total, (1, 128))
    count_out[0] = own_count
    counts[me] = own_count

    pl.semaphore_wait(barrier, devices - 1)

    def count_copy(step):
        return pltpu.make_async_remote_copy(
            src_ref=count_out.at[0],
            dst_ref=counts.at[me],
            send_sem=count_send.at[step],
            recv_sem=count_recv.at[me],
            device_id=place(after(step)),
            device_id_type=MESH,
        )

    def count_from(step):
        source = ahead(step)
        return pltpu.make_async_remote_copy(
            src_ref=count_out.at[0],
            dst_ref=counts.at[source],
            send_sem=count_send.at[step],
            recv_sem=count_recv.at[source],
            device_id=place(source),
            device_id_type=MESH,
        )

    def send_count(step, carry):
        count_copy(step).start()
        return carry

    lax.fori_loop(1, devices, send_count, 0)

    rank = jnp.where(jnp.sum(path.astype(jnp.float32), axis=0, keepdims=True) > 0, depth, -1)
    for r in range(requests):
        rank = jnp.where((group == r) & (rank >= 0), rank + starts[r], rank)
    load.wait()
    folded = jnp.zeros((block * FOLD, slab), jnp.float32)
    for piece in range(FOLD):
        take = one_hot(block * FOLD, jnp.where(rank >= 0, rank * FOLD + piece, -1))
        part = hidden[:, :, piece * slab : (piece + 1) * slab].reshape(every, slab)
        folded = folded + jnp.dot(take, part, preferred_element_type=jnp.float32)
    staged[0:block] = folded.astype(jnp.bfloat16).reshape(block, FOLD, slab)
    staged[block] = jnp.zeros((FOLD, slab), jnp.bfloat16)

    def await_count(step, carry):
        count_from(step).wait_recv()
        return carry

    lax.fori_loop(1, devices, await_count, 0)

    every_count = counts[...].reshape(devices, 128)
    source = lax.broadcasted_iota(jnp.int32, (devices, 128), 0)
    before_row = jnp.sum(jnp.where(source < me, every_count, 0).astype(jnp.float32), axis=0, keepdims=True)
    before_row = before_row.astype(jnp.int32)
    before = before_row[0, 0]

    for peer in range(devices):
        turn = mod(peer + devices * block * devices - before, devices)
        outgoing[peer] = staged[jnp.minimum(turn, block)]

    def row_copy(step):
        peer = after(step)
        return pltpu.make_async_remote_copy(
            src_ref=outgoing.at[peer],
            dst_ref=incoming.at[me],
            send_sem=row_send.at[step],
            recv_sem=row_recv.at[me],
            device_id=place(peer),
            device_id_type=MESH,
        )

    def row_from(step):
        origin = ahead(step)
        return pltpu.make_async_remote_copy(
            src_ref=outgoing.at[origin],
            dst_ref=incoming.at[origin],
            send_sem=row_send.at[step],
            recv_sem=row_recv.at[origin],
            device_id=place(origin),
            device_id_type=MESH,
        )

    def send_row(step, carry):
        row_copy(step).start()
        return carry

    lax.fori_loop(1, devices, send_row, 0)
    keep = pltpu.make_async_copy(outgoing.at[me], incoming.at[me], own_sem)
    keep.start()

    column = lax.broadcasted_iota(jnp.int32, (devices, devices * FOLD), 1)
    owner = lax.broadcasted_iota(jnp.int32, (devices, devices * FOLD), 0)
    wide = jnp.concatenate([every_count] * (devices * FOLD // 128), axis=1).astype(jnp.float32)
    of = div(column, FOLD)
    first = jnp.sum(jnp.where(owner < of, wide, 0.0), axis=0, keepdims=True).astype(jnp.int32)
    amount = jnp.sum(jnp.where(owner == of, wide, 0.0), axis=0, keepdims=True).astype(jnp.int32)
    turn = mod(me + devices * block * devices - first, devices)
    piece = mod(lax.broadcasted_iota(jnp.int32, (1, devices * FOLD), 1), FOLD)
    slot = div(first + turn, devices)
    placing = one_hot(block * FOLD, jnp.where(turn < amount, piece * block + slot, -1))

    tokens = lanes_of(tokens_ref[...])
    chosen = jnp.sum(jnp.where(best_hot, tokens, 0).astype(jnp.float32), axis=1, keepdims=True)
    chosen = chosen.astype(jnp.int32)
    for r in range(requests):
        length_ref[r] = length[r, 0]
        offsets_ref[r] = starts[r][0, 0] + before
        next_ref[r] = chosen[r, 0]

    keep.wait()

    def await_row(step, carry):
        row_from(step).wait_recv()
        return carry

    lax.fori_loop(1, devices, await_row, 0)
    rows = incoming[...].reshape(devices * FOLD, slab)
    placed = jnp.dot(placing, rows, preferred_element_type=jnp.float32).astype(jnp.bfloat16)
    for part in range(FOLD):
        dest_ref[:, part * slab : (part + 1) * slab] = placed[part * block : (part + 1) * block, :]

    def drain(step, carry):
        count_copy(step).wait_send()
        row_copy(step).wait_send()
        return carry

    lax.fori_loop(1, devices, drain, 0)


def solution(mesh):
    n_gx, n_gy = mesh.shape["gx"], mesh.shape["gy"]
    devices = n_gx * n_gy

    def local(hidden, parents, accepted, token_ids):
        requests, nodes, width = hidden.shape
        block = requests * DEPTH
        slab = width // FOLD
        vmem = pl.BlockSpec(memory_space=pltpu.VMEM)
        smem = pl.BlockSpec(memory_space=pltpu.SMEM)
        small = jax.ShapeDtypeStruct((requests,), jnp.int32)
        return pl.pallas_call(
            functools.partial(kernel, (n_gx, n_gy, requests, nodes, width, block)),
            out_shape=(jax.ShapeDtypeStruct((block, width), hidden.dtype), small, small, small),
            in_specs=[pl.BlockSpec(memory_space=pl.ANY), vmem, vmem, vmem],
            out_specs=(vmem, smem, smem, smem),
            scratch_shapes=[
                pltpu.VMEM(hidden.shape, hidden.dtype),
                pltpu.VMEM((block + 1, FOLD, slab), hidden.dtype),
                pltpu.VMEM((devices, FOLD, slab), hidden.dtype),
                pltpu.VMEM((devices, FOLD, slab), hidden.dtype),
                pltpu.VMEM((1, 1, 128), jnp.int32),
                pltpu.VMEM((devices, 1, 128), jnp.int32),
                pltpu.SemaphoreType.DMA,
                pltpu.SemaphoreType.DMA,
                pltpu.SemaphoreType.DMA((devices,)),
                pltpu.SemaphoreType.DMA((devices,)),
                pltpu.SemaphoreType.DMA((devices,)),
                pltpu.SemaphoreType.DMA((devices,)),
            ],
            compiler_params=pltpu.CompilerParams(collective_id=0, has_side_effects=True),
        )(hidden, parents, accepted, token_ids)

    placed = (
        P(("gx", "gy"), None, None),
        P(("gx", "gy"), None),
        P(("gx", "gy"), None),
        P(("gx", "gy"), None),
    )
    return jax.shard_map(
        local,
        mesh=mesh,
        in_specs=placed,
        out_specs=(P(("gx", "gy"), None), P(("gx", "gy")), P(("gx", "gy")), P(("gx", "gy"))),
        check_vma=False,
    )
```

time: 96.9 us -> 27.9 us (0.29)
  blocking collectives: 41.9 us -> 0 us
  other arithmetic: 28.9 us -> 0 us
  Pallas kernels: 0 us -> 22 us
  starting transfers between devices: 10.2 us -> 0 us
  waiting for transfers between devices: 9.78 us -> 0 us
  local copies, waits for them, and re-layouts: 2.62 us -> 5.07 us
  matrix products: 1.62 us -> 0 us
    unnamed x1 -> x0, blocking collectives: 41.9 us -> none
    pallas_call x0 -> x1, Pallas kernels: none -> 22 us  [local(): pl.pallas_call(functools.partial(kernel, (n_gx, n_gy, requests, nodes, wi...]
    reduce_sum x17 -> x0, other arithmetic: 15.7 us -> none  [the longest x15 14.5 us: pick_from(): return jnp.sum(jnp.where(hot, table, 0), axis=-1)]
    all_to_all x2 -> x0, starting transfers between devices: 10.2 us -> none  [the longest x1 5.83 us: local(): lax.all_to_all(outgoing, ('gx', 'gy'), split_axis=0, concat_axis=0, tiled...]
    all_to_all x2 -> x0, waiting for transfers between devices: 9.78 us -> none  [the longest x1 9.78 us: local(): lax.all_to_all(outgoing, ('gx', 'gy'), split_axis=0, concat_axis=0, tiled...]
    select_n x9 -> x0, other arithmetic: 5.54 us -> none  [the longest x7 4.87 us: tree_walk(): alive = jnp.where(is_root, 1, accepted * alive_up)]
    unnamed x8 -> x4, local copies, waits for them, and re-layouts: 1.92 us -> 5.07 us
    convert_element_type x1 -> x0, other arithmetic: 2.04 us -> none  [local(): jnp.where(valid, (before + peer_rank) // devices + 1, 0)]
  transfers between devices with their start and end apart: 2 -> 0, of which waited for: 1 -> 0; matrix products, arithmetic and copies ran while one was open for 13% -> 0% of each run, Pallas kernels for 0% -> 0%
where the time goes in v1:
time: 27.9 us; the launch traced here: 27.7 us
  Pallas kernels  22 us (79%)
  local copies, waits for them, and re-layouts  5.07 us (18%)
  between operations  0.64 us (2%)
    pallas_call x1, Pallas kernels, local(): pl.pallas_call(functools.partial(kernel, (n_gx, n_gy, requests, nodes, wi...  22 us
    unnamed x4, local copies, waits for them, and re-layouts  5.07 us

profile of v1, /device:TPU:0, one launch (start us, length us, event | category | flops | bytes accessed | tf_op | source)
XLA Modules:
  0.0 27.7 jit_solution(6598455162328510609)
XLA Ops:
  0.6 22.0 %shard_map.75 = (bf16[32,4096]{1,0:T(8,128)(2,1)}, s32[4]{0:T(128)}, s32[4]{0:T(128)}, s32[4]{0:T(128)}) custom-call(bf16[4,64,4096]{2,1,0:T(8,128)(2,1)} %hidden_ref.1, s32[4,64]{1,0:T(4,128)} %parents_ref.1, s32[4,64]{1,0:T(4,128)} %accepted_ref.1, s32[4,64]{1,0:T(4,128)} %tokens_ref.1), custom_call_target="tpu_custom_call" | custom-call | tf_op jit(solution)/shard_map/pallas_call | solution.py:262
  22.7 1.7 %copy.12 = bf16[32,4096]{1,0:T(8,128)(2,1)} copy(bf16[32,4096]{1,0:T(8,128)(2,1)} %get-tuple-element.8) | data formatting | bytes 524288
  24.3 1.1 %copy.13 = s32[4]{0:T(128)} copy(s32[4]{0:T(128)} %get-tuple-element.9) | data formatting | bytes 32
  25.5 1.1 %copy.14 = s32[4]{0:T(128)} copy(s32[4]{0:T(128)} %get-tuple-element.10) | data formatting | bytes 32
  26.5 1.2 %copy.15 = s32[4]{0:T(128)} copy(s32[4]{0:T(128)} %get-tuple-element.11) | data formatting | bytes 32

commit v2 on v1

v2 whole, which is shorter than its diff:
```python
import functools

import jax
import jax.numpy as jnp
from jax import lax
from jax.experimental import pallas as pl
from jax.experimental.pallas import tpu as pltpu
from jax.sharding import PartitionSpec as P

DEPTH = 8
FOLD = 16
MESH = pl.DeviceIdType.MESH


def mod(value, size):
    return value & (size - 1) if size & (size - 1) == 0 else lax.rem(value, size)


def div(value, size):
    if size & (size - 1) == 0:
        return lax.shift_right_logical(value, jnp.int32(size.bit_length() - 1) + jnp.zeros_like(value))
    return lax.div(value, jnp.int32(size) + jnp.zeros_like(value))


def lanes_of(table):
    return jnp.concatenate([table[r : r + 1, :] for r in range(table.shape[0])], axis=1)


def one_hot(rows, target):
    shape = (rows, target.shape[1])
    return (lax.broadcasted_iota(jnp.int32, shape, 0) == target).astype(jnp.bfloat16)


def kernel(
    sizes,
    hidden_ref,
    parents_ref,
    accepted_ref,
    tokens_ref,
    dest_ref,
    length_ref,
    offsets_ref,
    next_ref,
    hidden,
    parents_in,
    accepted_in,
    tokens_in,
    staged,
    outgoing,
    incoming,
    count_out,
    near_counts,
    counts,
    load_sem,
    small_sem,
    own_sem,
    near_send,
    near_recv,
    far_send,
    far_recv,
    row_send,
    row_recv,
):
    n_gx, n_gy, requests, nodes, width, block = sizes
    devices = n_gx * n_gy
    slab = width // FOLD
    every = requests * nodes
    at_gx, at_gy = lax.axis_index("gx"), lax.axis_index("gy")
    me = at_gx * n_gy + at_gy
    near = [(lax.rem(at_gx + step, n_gx), at_gy) for step in range(1, n_gx)]
    far = [(at_gx, lax.rem(at_gy + step, n_gy)) for step in range(1, n_gy)]

    barrier = pltpu.get_barrier_semaphore()
    for partner in far + near:
        pl.semaphore_signal(barrier, inc=1, device_id=partner, device_id_type=MESH)
    loads = [
        pltpu.make_async_copy(parents_ref, parents_in, small_sem.at[0]),
        pltpu.make_async_copy(accepted_ref, accepted_in, small_sem.at[1]),
        pltpu.make_async_copy(tokens_ref, tokens_in, small_sem.at[2]),
        pltpu.make_async_copy(hidden_ref, hidden, load_sem),
    ]
    for load in loads:
        load.start()
    for load in loads[:3]:
        load.wait()

    lane = lax.broadcasted_iota(jnp.int32, (1, every), 1)
    group = div(lane, nodes)
    parents = lanes_of(parents_in[...])
    bad = (parents >= 0) & (lanes_of(accepted_in[...]) == 0)
    up = jnp.where(parents < 0, -1, parents + group * nodes)
    row = lax.broadcasted_iota(jnp.int32, (every, every), 0)
    col = lax.broadcasted_iota(jnp.int32, (every, every), 1)
    step_up = ((row == up) | (row == col)).astype(jnp.bfloat16)
    reach = step_up
    hops = 1
    while hops < DEPTH - 1:
        reach = jnp.dot(reach, reach, preferred_element_type=jnp.float32).astype(jnp.bfloat16)
        hops *= 2
    reach = (reach > 0).astype(jnp.bfloat16)
    which = lax.broadcasted_iota(jnp.int32, (16, every), 0)
    probe = jnp.where(which == 0, 1.0, jnp.where(bad, 1.0, 0.0)).astype(jnp.bfloat16)
    tally = jnp.dot(probe, reach, preferred_element_type=jnp.float32).astype(jnp.int32)
    depth = tally[0:1, :] - 1
    alive = tally[1:2, :] == 0
    score = jnp.where(alive, depth * nodes + (nodes - 1 - mod(lane, nodes)), -1)
    pad = 16
    mine = lax.broadcasted_iota(jnp.int32, (pad, every), 0) == group
    scores = jnp.where(mine, score, -1)
    top = jnp.max(scores.astype(jnp.float32), axis=1, keepdims=True).astype(jnp.int32)
    best_hot = mine & (scores == top)
    path = lax.dot_general(
        jnp.where(best_hot, 1.0, 0.0).astype(jnp.bfloat16),
        reach,
        (((1,), (1,)), ((), ())),
        preferred_element_type=jnp.float32,
    ).astype(jnp.int32)
    request = lax.broadcasted_iota(jnp.int32, (pad, 1), 0)
    length = jnp.where(request < requests, div(jnp.maximum(top, 0), nodes) + 1, 0)
    starts = []
    total = jnp.zeros((1, 1), jnp.int32)
    for r in range(requests):
        starts.append(total)
        total = total + length[r : r + 1, :]

    own_count = jnp.broadcast_to(total, (1, 128))
    count_out[0] = own_count
    near_counts[at_gx] = own_count

    pl.semaphore_wait(barrier, n_gx + n_gy - 2)

    near_copies = [
        pltpu.make_async_remote_copy(
            src_ref=count_out.at[0],
            dst_ref=near_counts.at[at_gx],
            send_sem=near_send,
            recv_sem=near_recv,
            device_id=partner,
            device_id_type=MESH,
        )
        for partner in near
    ]
    for copy in near_copies:
        copy.start()

    rank = jnp.where(jnp.sum(path.astype(jnp.float32), axis=0, keepdims=True) > 0, depth, -1)
    for r in range(requests):
        rank = jnp.where((group == r) & (rank >= 0), rank + starts[r], rank)
    def arrived(ref, amount, sem):
        part = ref.at[pl.ds(0, amount)]
        pltpu.make_async_copy(part, part, sem).wait()

    arrived(near_counts, n_gx - 1, near_recv)
    counts[at_gy] = near_counts[...]
    far_copies = [
        pltpu.make_async_remote_copy(
            src_ref=near_counts,
            dst_ref=counts.at[at_gy],
            send_sem=far_send,
            recv_sem=far_recv,
            device_id=partner,
            device_id_type=MESH,
        )
        for partner in far
    ]
    for copy in far_copies:
        copy.start()

    loads[3].wait()
    folded = jnp.zeros((block * FOLD, slab), jnp.float32)
    for piece in range(FOLD):
        take = one_hot(block * FOLD, jnp.where(rank >= 0, rank * FOLD + piece, -1))
        part = hidden[:, :, piece * slab : (piece + 1) * slab].reshape(every, slab)
        folded = folded + jnp.dot(take, part, preferred_element_type=jnp.float32)
    staged[0:block] = folded.astype(jnp.bfloat16).reshape(block, FOLD, slab)
    staged[block] = jnp.zeros((FOLD, slab), jnp.bfloat16)

    arrived(counts, n_gy - 1, far_recv)

    every_count = counts[...].reshape(devices, 128)

    def source_of(index):
        return mod(index, n_gx) * n_gy + div(index, n_gx)

    source = source_of(lax.broadcasted_iota(jnp.int32, (devices, 128), 0))
    before_row = jnp.sum(jnp.where(source < me, every_count, 0).astype(jnp.float32), axis=0, keepdims=True)
    before_row = before_row.astype(jnp.int32)
    before = before_row[0, 0]

    for peer in range(devices):
        turn = mod(peer + devices * block * devices - before, devices)
        outgoing[peer] = staged[jnp.minimum(turn, block)]

    row_copies = []
    for step in range(1, devices):
        peer = lax.rem(me + step, devices)
        row_copies.append(
            pltpu.make_async_remote_copy(
                src_ref=outgoing.at[peer],
                dst_ref=incoming.at[me],
                send_sem=row_send,
                recv_sem=row_recv,
                device_id=(lax.div(peer, n_gy), lax.rem(peer, n_gy)),
                device_id_type=MESH,
            )
        )
    for copy in row_copies:
        copy.start()
    keep = pltpu.make_async_copy(outgoing.at[me], incoming.at[me], own_sem)
    keep.start()

    column = lax.broadcasted_iota(jnp.int32, (devices, devices * FOLD), 1)
    owner = source_of(lax.broadcasted_iota(jnp.int32, (devices, devices * FOLD), 0))
    wide = jnp.concatenate([every_count] * (devices * FOLD // 128), axis=1).astype(jnp.float32)
    of = div(column, FOLD)
    first = jnp.sum(jnp.where(owner < of, wide, 0.0), axis=0, keepdims=True).astype(jnp.int32)
    amount = jnp.sum(jnp.where(owner == of, wide, 0.0), axis=0, keepdims=True).astype(jnp.int32)
    turn = mod(me + devices * block * devices - first, devices)
    piece = mod(lax.broadcasted_iota(jnp.int32, (1, devices * FOLD), 1), FOLD)
    slot = div(first + turn, devices)
    placing = one_hot(block * FOLD, jnp.where(turn < amount, piece * block + slot, -1))

    tokens = lanes_of(tokens_in[...])
    chosen = jnp.sum(jnp.where(best_hot, tokens, 0).astype(jnp.float32), axis=1, keepdims=True)
    chosen = chosen.astype(jnp.int32)
    for r in range(requests):
        length_ref[r] = length[r, 0]
        offsets_ref[r] = starts[r][0, 0] + before
        next_ref[r] = chosen[r, 0]

    keep.wait()

    arrived(incoming, devices - 1, row_recv)
    rows = incoming[...].reshape(devices * FOLD, slab)
    placed = jnp.dot(placing, rows, preferred_element_type=jnp.float32).astype(jnp.bfloat16)
    for part in range(FOLD):
        dest_ref[:, part * slab : (part + 1) * slab] = placed[part * block : (part + 1) * block, :]

    arrived(near_counts, n_gx - 1, near_send)
    arrived(counts, n_gy - 1, far_send)
    arrived(incoming, devices - 1, row_send)


def hand_on(*refs):
    half = (len(refs) - 1) // 2
    sems = refs[-1]
    copies = [pltpu.make_async_copy(refs[i], refs[half + i], sems.at[i]) for i in range(half)]
    for copy in copies:
        copy.start()
    for copy in copies:
        copy.wait()


def solution(mesh):
    n_gx, n_gy = mesh.shape["gx"], mesh.shape["gy"]
    devices = n_gx * n_gy

    def local(hidden, parents, accepted, token_ids):
        requests, nodes, width = hidden.shape
        block = requests * DEPTH
        slab = width // FOLD
        vmem = pl.BlockSpec(memory_space=pltpu.VMEM)
        smem = pl.BlockSpec(memory_space=pltpu.SMEM)
        small = jax.ShapeDtypeStruct((requests,), jnp.int32)
        anywhere = pl.BlockSpec(memory_space=pl.ANY)
        outs = (jax.ShapeDtypeStruct((block, width), hidden.dtype), small, small, small)
        results = pl.pallas_call(
            functools.partial(kernel, (n_gx, n_gy, requests, nodes, width, block)),
            out_shape=outs,
            in_specs=[pl.BlockSpec(memory_space=pltpu.HBM)] * 4,
            out_specs=(vmem, smem, smem, smem),
            scratch_shapes=[
                pltpu.VMEM(hidden.shape, hidden.dtype),
                pltpu.VMEM((requests, nodes), jnp.int32),
                pltpu.VMEM((requests, nodes), jnp.int32),
                pltpu.VMEM((requests, nodes), jnp.int32),
                pltpu.VMEM((block + 1, FOLD, slab), hidden.dtype),
                pltpu.VMEM((devices, FOLD, slab), hidden.dtype),
                pltpu.VMEM((devices, FOLD, slab), hidden.dtype),
                pltpu.VMEM((1, 1, 128), jnp.int32),
                pltpu.VMEM((n_gx, 1, 128), jnp.int32),
                pltpu.VMEM((n_gy, n_gx, 1, 128), jnp.int32),
                pltpu.SemaphoreType.DMA,
                pltpu.SemaphoreType.DMA((3,)),
                pltpu.SemaphoreType.DMA,
                pltpu.SemaphoreType.DMA,
                pltpu.SemaphoreType.DMA,
                pltpu.SemaphoreType.DMA,
                pltpu.SemaphoreType.DMA,
                pltpu.SemaphoreType.DMA,
                pltpu.SemaphoreType.DMA,
            ],
            compiler_params=pltpu.CompilerParams(
                collective_id=0, has_side_effects=True, vmem_limit_bytes=24 << 20
            ),
        )(hidden, parents, accepted, token_ids)
        return pl.pallas_call(
            hand_on,
            out_shape=outs,
            in_specs=[anywhere] * len(outs),
            out_specs=(anywhere,) * len(outs),
            scratch_shapes=[pltpu.SemaphoreType.DMA((len(outs),))],
            compiler_params=pltpu.CompilerParams(vmem_limit_bytes=1 << 20),
        )(*results)

    placed = (
        P(("gx", "gy"), None, None),
        P(("gx", "gy"), None),
        P(("gx", "gy"), None),
        P(("gx", "gy"), None),
    )
    return jax.shard_map(
        local,
        mesh=mesh,
        in_specs=placed,
        out_specs=(P(("gx", "gy"), None), P(("gx", "gy")), P(("gx", "gy")), P(("gx", "gy"))),
        check_vma=False,
    )
```

time: 27.9 us -> 26.2 us (0.939)
  local copies, waits for them, and re-layouts: 5.07 us -> 3.63 us
  Pallas kernels: 22 us -> 21.7 us
    unnamed x4 -> x8, local copies, waits for them, and re-layouts: 5.07 us -> 3.63 us
    pallas_call x1, Pallas kernels: 22 us -> 20.9 us  [local(): pl.pallas_call(functools.partial(kernel, (n_gx, n_gy, requests, nodes, wi...]
    pallas_call x0 -> x1, Pallas kernels: none -> 0.75 us  [local(): pl.pallas_call(hand_on, out_shape=outs, in_specs=[anywhere] * len(outs),...]
where the time goes in v2:
time: 26.2 us; the launch traced here: 26 us
  Pallas kernels  21.7 us (83%)
  local copies, waits for them, and re-layouts  3.63 us (14%)
  between operations  0.65 us (2%)
    pallas_call x1, Pallas kernels, local(): pl.pallas_call(functools.partial(kernel, (n_gx, n_gy, requests, nodes, wi...  20.9 us
    unnamed x8, local copies, waits for them, and re-layouts  3.63 us
    pallas_call x1, Pallas kernels, local(): pl.pallas_call(hand_on, out_shape=outs, in_specs=[anywhere] * len(outs),...  0.75 us

profile of v2, /device:TPU:0, one launch (start us, length us, event | category | flops | bytes accessed | tf_op | source)
XLA Modules:
  0.0 26.0 jit_solution(1548193254127786163)
XLA Ops:
  0.6 0.0 copy-start
  0.6 1.6 %copy-done = bf16[4,64,4096]{2,1,0:T(8,128)(2,1)S(1)} copy-done((bf16[4,64,4096]{2,1,0:T(8,128)(2,1)S(1)}, bf16[4,64,4096]{2,1,0:T(8,128)(2,1)}, u32[]{:S(2)}) %copy-start) | copy-done | bytes 2097176
  2.2 0.0 copy-start.1
  2.2 0.7 %copy-done.1 = s32[4,64]{1,0:T(4,128)S(1)} copy-done((s32[4,64]{1,0:T(4,128)S(1)}, s32[4,64]{1,0:T(4,128)}, u32[]{:S(2)}) %copy-start.1) | copy-done | bytes 1048
  2.9 0.0 copy-start.2
  2.9 0.7 %copy-done.2 = s32[4,64]{1,0:T(4,128)S(1)} copy-done((s32[4,64]{1,0:T(4,128)S(1)}, s32[4,64]{1,0:T(4,128)}, u32[]{:S(2)}) %copy-start.2) | copy-done | bytes 1048
  3.6 0.0 copy-start.3
  3.6 0.7 %copy-done.3 = s32[4,64]{1,0:T(4,128)S(1)} copy-done((s32[4,64]{1,0:T(4,128)S(1)}, s32[4,64]{1,0:T(4,128)}, u32[]{:S(2)}) %copy-start.3) | copy-done | bytes 1048
  4.3 20.9 %shard_map.75 = (bf16[32,4096]{1,0:T(8,128)(2,1)S(1)}, s32[4]{0:T(128)S(1)}, s32[4]{0:T(128)S(1)}, s32[4]{0:T(128)S(1)}) custom-call(bf16[4,64,4096]{2,1,0:T(8,128)(2,1)S(1)} %copy-done, s32[4,64]{1,0:T(4,128)S(1)} %copy-done.1, s32[4,64]{1,0:T(4,128)S(1)} %copy-done.2, s32[4,64]{1,0:T(4,128)S(1)} %copy-done.3), custom_call_target="tpu_custom_call" | custom-call | tf_op jit(solution)/shard_map/pallas_call | solution.py:267
  25.2 0.7 %shard_map.76 = (bf16[32,4096]{1,0:T(8,128)(2,1)}, s32[4]{0:T(128)}, s32[4]{0:T(128)}, s32[4]{0:T(128)}) custom-call(bf16[32,4096]{1,0:T(8,128)(2,1)S(1)} %get-tuple-element.8.refs_0_, s32[4]{0:T(128)S(1)} %get-tuple-element.9.refs_1_, s32[4]{0:T(128)S(1)} %get-tuple-element.10.refs_2_, s32[4]{0:T(128)S(1)} %get-tuple-element.11.refs_3_), custom_call_target="tpu_custom_call" | custom-call | tf_op jit(solution)/shard_map/pallas_call | solution.py:297
Async XLA Ops:
  0.6 1.6 %copy-start = (bf16[4,64,4096]{2,1,0:T(8,128)(2,1)S(1)}, bf16[4,64,4096]{2,1,0:T(8,128)(2,1)}, u32[]{:S(2)}) copy-start(bf16[4,64,4096]{2,1,0:T(8,128)(2,1)} %hidden_ref.1) | copy-start | bytes 6291460
  2.2 0.7 %copy-start.1 = (s32[4,64]{1,0:T(4,128)S(1)}, s32[4,64]{1,0:T(4,128)}, u32[]{:S(2)}) copy-start(s32[4,64]{1,0:T(4,128)} %parents_ref.1) | copy-start | bytes 3076
  2.9 0.7 %copy-start.2 = (s32[4,64]{1,0:T(4,128)S(1)}, s32[4,64]{1,0:T(4,128)}, u32[]{:S(2)}) copy-start(s32[4,64]{1,0:T(4,128)} %accepted_ref.1) | copy-start | bytes 3076
  3.6 0.7 %copy-start.3 = (s32[4,64]{1,0:T(4,128)S(1)}, s32[4,64]{1,0:T(4,128)}, u32[]{:S(2)}) copy-start(s32[4,64]{1,0:T(4,128)} %tokens_ref.1) | copy-start | bytes 3076

commit v3 on v2

--- a/solution.py
+++ b/solution.py
@@ -293,7 +293,7 @@
             compiler_params=pltpu.CompilerParams(
                 collective_id=0, has_side_effects=True, vmem_limit_bytes=24 << 20
             ),
-        )(hidden, parents, accepted, token_ids)
+        )(*[pltpu.with_memory_space_constraint(x, pltpu.HBM) for x in (hidden, parents, accepted, token_ids)])
         return pl.pallas_call(
             hand_on,
             out_shape=outs,

time: 26.2 us -> 22.5 us (0.86)
  local copies, waits for them, and re-layouts: 3.63 us -> 0 us
    unnamed x8 -> x0, local copies, waits for them, and re-layouts: 3.63 us -> none
where the time goes in v3:
time: 22.5 us; the launch traced here: 22.4 us
  Pallas kernels  21.7 us (96%)
  between operations  0.64 us (3%)
    pallas_call x1, Pallas kernels, local(): pl.pallas_call(functools.partial(kernel, (n_gx, n_gy, requests, nodes, wi...  21 us
    pallas_call x1, Pallas kernels, local(): pl.pallas_call(hand_on, out_shape=outs, in_specs=[anywhere] * len(outs),...  0.75 us

profile of v3, /device:TPU:0, one launch (start us, length us, event | category | flops | bytes accessed | tf_op | source)
XLA Modules:
  0.0 22.4 jit_solution(6638025353122340587)
XLA Ops:
  0.6 21.0 %shard_map.75 = (bf16[32,4096]{1,0:T(8,128)(2,1)S(1)}, s32[4]{0:T(128)S(1)}, s32[4]{0:T(128)S(1)}, s32[4]{0:T(128)S(1)}) custom-call(bf16[4,64,4096]{2,1,0:T(8,128)(2,1)} %hidden_ref.1, s32[4,64]{1,0:T(4,128)} %parents_ref.1, s32[4,64]{1,0:T(4,128)} %accepted_ref.1, s32[4,64]{1,0:T(4,128)} %tokens_ref.1), custom_call_target="tpu_custom_call" | custom-call | tf_op jit(solution)/shard_map/pallas_call | solution.py:267
  21.6 0.7 %shard_map.76 = (bf16[32,4096]{1,0:T(8,128)(2,1)}, s32[4]{0:T(128)}, s32[4]{0:T(128)}, s32[4]{0:T(128)}) custom-call(bf16[32,4096]{1,0:T(8,128)(2,1)S(1)} %get-tuple-element.8.refs_0_, s32[4]{0:T(128)S(1)} %get-tuple-element.9.refs_1_, s32[4]{0:T(128)S(1)} %get-tuple-element.10.refs_2_, s32[4]{0:T(128)S(1)} %get-tuple-element.11.refs_3_), custom_call_target="tpu_custom_call" | custom-call | tf_op jit(solution)/shard_map/pallas_call | solution.py:297

commit v4 on v3

--- a/solution.py
+++ b/solution.py
@@ -49,15 +49,12 @@
     outgoing,
     incoming,
     count_out,
-    near_counts,
     counts,
     load_sem,
     small_sem,
     own_sem,
-    near_send,
-    near_recv,
-    far_send,
-    far_recv,
+    count_send,
+    count_recv,
     row_send,
     row_recv,
 ):
@@ -65,14 +62,19 @@
     devices = n_gx * n_gy
     slab = width // FOLD
     every = requests * nodes
-    at_gx, at_gy = lax.axis_index("gx"), lax.axis_index("gy")
-    me = at_gx * n_gy + at_gy
-    near = [(lax.rem(at_gx + step, n_gx), at_gy) for step in range(1, n_gx)]
-    far = [(at_gx, lax.rem(at_gy + step, n_gy)) for step in range(1, n_gy)]
+    me = lax.axis_index("gx") * n_gy + lax.axis_index("gy")
+
+    def others(order):
+        if devices & (devices - 1):
+            return [lax.rem(me + step, devices) for step in order]
+        return [me ^ step for step in order]
+
+    def place(index):
+        return (div(index, n_gy), mod(index, n_gy))
 
     barrier = pltpu.get_barrier_semaphore()
-    for partner in far + near:
-        pl.semaphore_signal(barrier, inc=1, device_id=partner, device_id_type=MESH)
+    for peer in others(range(devices - 1, 0, -1)):
+        pl.semaphore_signal(barrier, inc=1, device_id=place(peer), device_id_type=MESH)
     loads = [
         pltpu.make_async_copy(parents_ref, parents_in, small_sem.at[0]),
         pltpu.make_async_copy(accepted_ref, accepted_in, small_sem.at[1]),
@@ -84,87 +86,79 @@
     for load in loads[:3]:
         load.wait()
 
+    def padded(table, fill):
+        wide = jnp.concatenate([table, jnp.full((requests, 128 - nodes), fill, jnp.int32)], axis=1)
+        return jnp.concatenate([wide, jnp.full((8 - requests, 128), fill, jnp.int32)], axis=0)
+
+    parents = padded(parents_in[...], -1)
+    accepted = padded(accepted_in[...], 1)
+    at_node = lax.broadcasted_iota(jnp.int32, (8, 128), 1)
+    request = lax.broadcasted_iota(jnp.int32, (8, 128), 0)
+    jump = jnp.where(parents < 0, at_node, parents)
+    tally = jnp.where(parents < 0, 0, jnp.where(accepted == 0, nodes + 1, 1))
+    hops = 1
+    while hops < DEPTH - 1:
+        tally = tally + jnp.take_along_axis(tally, jump, axis=1, mode="promise_in_bounds")
+        hops *= 2
+        if hops < DEPTH - 1:
+            jump = jnp.take_along_axis(jump, jump, axis=1, mode="promise_in_bounds")
+    real = (at_node < nodes) & (request < requests)
+    level = mod(tally, nodes)
+    score = jnp.where(real & (tally < nodes), level * nodes + (nodes - 1 - at_node), -1)
+    top = jnp.max(score.astype(jnp.float32), axis=1, keepdims=True).astype(jnp.int32)
+    length = jnp.where(top >= 0, div(jnp.maximum(top, 0), nodes) + 1, 0)
+    starts = []
+    total = jnp.zeros((1, 1), jnp.int32)
+    for r in range(requests):
+        starts.append(total)
+        total = total + length[r : r + 1, :]
+
+    own_count = jnp.broadcast_to(total, (1, 128))
+    count_out[0] = own_count
+    counts[me] = own_count
+
+    pl.semaphore_wait(barrier, devices - 1)
+
+    count_copies = [
+        pltpu.make_async_remote_copy(
+            src_ref=count_out.at[0],
+            dst_ref=counts.at[me],
+            send_sem=count_send,
+            recv_sem=count_recv,
+            device_id=place(peer),
+            device_id_type=MESH,
+        )
+        for peer in others(range(devices - 1, 0, -1))
+    ]
+    for copy in count_copies:
+        copy.start()
+
     lane = lax.broadcasted_iota(jnp.int32, (1, every), 1)
     group = div(lane, nodes)
-    parents = lanes_of(parents_in[...])
-    bad = (parents >= 0) & (lanes_of(accepted_in[...]) == 0)
-    up = jnp.where(parents < 0, -1, parents + group * nodes)
+    above = lanes_of(parents_in[...])
+    up = jnp.where(above < 0, -1, above + group * nodes)
     row = lax.broadcasted_iota(jnp.int32, (every, every), 0)
     col = lax.broadcasted_iota(jnp.int32, (every, every), 1)
-    step_up = ((row == up) | (row == col)).astype(jnp.bfloat16)
-    reach = step_up
+    reach = ((row == up) | (row == col)).astype(jnp.bfloat16)
     hops = 1
     while hops < DEPTH - 1:
         reach = jnp.dot(reach, reach, preferred_element_type=jnp.float32).astype(jnp.bfloat16)
         hops *= 2
     reach = (reach > 0).astype(jnp.bfloat16)
-    which = lax.broadcasted_iota(jnp.int32, (16, every), 0)
-    probe = jnp.where(which == 0, 1.0, jnp.where(bad, 1.0, 0.0)).astype(jnp.bfloat16)
-    tally = jnp.dot(probe, reach, preferred_element_type=jnp.float32).astype(jnp.int32)
-    depth = tally[0:1, :] - 1
-    alive = tally[1:2, :] == 0
-    score = jnp.where(alive, depth * nodes + (nodes - 1 - mod(lane, nodes)), -1)
-    pad = 16
-    mine = lax.broadcasted_iota(jnp.int32, (pad, every), 0) == group
-    scores = jnp.where(mine, score, -1)
-    top = jnp.max(scores.astype(jnp.float32), axis=1, keepdims=True).astype(jnp.int32)
-    best_hot = mine & (scores == top)
+    best = nodes - 1 - mod(jnp.maximum(top, 0), nodes)
+    ends = (lane == best + request[:, 0:1] * nodes) & (top >= 0)
+    ends = jnp.concatenate([ends.astype(jnp.float32), jnp.zeros((8, every), jnp.float32)], axis=0)
     path = lax.dot_general(
-        jnp.where(best_hot, 1.0, 0.0).astype(jnp.bfloat16),
-        reach,
-        (((1,), (1,)), ((), ())),
-        preferred_element_type=jnp.float32,
-    ).astype(jnp.int32)
-    request = lax.broadcasted_iota(jnp.int32, (pad, 1), 0)
-    length = jnp.where(request < requests, div(jnp.maximum(top, 0), nodes) + 1, 0)
-    starts = []
-    total = jnp.zeros((1, 1), jnp.int32)
-    for r in range(requests):
-        starts.append(total)
-        total = total + length[r : r + 1, :]
-
-    own_count = jnp.broadcast_to(total, (1, 128))
-    count_out[0] = own_count
-    near_counts[at_gx] = own_count
-
-    pl.semaphore_wait(barrier, n_gx + n_gy - 2)
-
-    near_copies = [
-        pltpu.make_async_remote_copy(
-            src_ref=count_out.at[0],
-            dst_ref=near_counts.at[at_gx],
-            send_sem=near_send,
-            recv_sem=near_recv,
-            device_id=partner,
-            device_id_type=MESH,
-        )
-        for partner in near
-    ]
-    for copy in near_copies:
-        copy.start()
-
-    rank = jnp.where(jnp.sum(path.astype(jnp.float32), axis=0, keepdims=True) > 0, depth, -1)
+        ends.astype(jnp.bfloat16), reach, (((1,), (1,)), ((), ())), preferred_element_type=jnp.float32
+    )
+    depth = lanes_of(level[0:requests, 0:nodes])
+
+    rank = jnp.where(jnp.sum(path, axis=0, keepdims=True) > 0, depth, -1)
     for r in range(requests):
         rank = jnp.where((group == r) & (rank >= 0), rank + starts[r], rank)
     def arrived(ref, amount, sem):
         part = ref.at[pl.ds(0, amount)]
         pltpu.make_async_copy(part, part, sem).wait()
-
-    arrived(near_counts, n_gx - 1, near_recv)
-    counts[at_gy] = near_counts[...]
-    far_copies = [
-        pltpu.make_async_remote_copy(
-            src_ref=near_counts,
-            dst_ref=counts.at[at_gy],
-            send_sem=far_send,
-            recv_sem=far_recv,
-            device_id=partner,
-            device_id_type=MESH,
-        )
-        for partner in far
-    ]
-    for copy in far_copies:
-        copy.start()
 
     loads[3].wait()
     folded = jnp.zeros((block * FOLD, slab), jnp.float32)
@@ -175,14 +169,10 @@
     staged[0:block] = folded.astype(jnp.bfloat16).reshape(block, FOLD, slab)
     staged[block] = jnp.zeros((FOLD, slab), jnp.bfloat16)
 
-    arrived(counts, n_gy - 1, far_recv)
+    arrived(counts, devices - 1, count_recv)
 
     every_count = counts[...].reshape(devices, 128)
-
-    def source_of(index):
-        return mod(index, n_gx) * n_gy + div(index, n_gx)
-
-    source = source_of(lax.broadcasted_iota(jnp.int32, (devices, 128), 0))
+    source = lax.broadcasted_iota(jnp.int32, (devices, 128), 0)
     before_row = jnp.sum(jnp.where(source < me, every_count, 0).astype(jnp.float32), axis=0, keepdims=True)
     before_row = before_row.astype(jnp.int32)
     before = before_row[0, 0]
@@ -191,26 +181,24 @@
         turn = mod(peer + devices * block * devices - before, devices)
         outgoing[peer] = staged[jnp.minimum(turn, block)]
 
-    row_copies = []
-    for step in range(1, devices):
-        peer = lax.rem(me + step, devices)
-        row_copies.append(
-            pltpu.make_async_remote_copy(
-                src_ref=outgoing.at[peer],
-                dst_ref=incoming.at[me],
-                send_sem=row_send,
-                recv_sem=row_recv,
-                device_id=(lax.div(peer, n_gy), lax.rem(peer, n_gy)),
-                device_id_type=MESH,
-            )
+    row_copies = [
+        pltpu.make_async_remote_copy(
+            src_ref=outgoing.at[peer],
+            dst_ref=incoming.at[me],
+            send_sem=row_send,
+            recv_sem=row_recv,
+            device_id=place(peer),
+            device_id_type=MESH,
         )
+        for peer in others(range(1, devices))
+    ]
     for copy in row_copies:
         copy.start()
     keep = pltpu.make_async_copy(outgoing.at[me], incoming.at[me], own_sem)
     keep.start()
 
     column = lax.broadcasted_iota(jnp.int32, (devices, devices * FOLD), 1)
-    owner = source_of(lax.broadcasted_iota(jnp.int32, (devices, devices * FOLD), 0))
+    owner = lax.broadcasted_iota(jnp.int32, (devices, devices * FOLD), 0)
     wide = jnp.concatenate([every_count] * (devices * FOLD // 128), axis=1).astype(jnp.float32)
     of = div(column, FOLD)
     first = jnp.sum(jnp.where(owner < of, wide, 0.0), axis=0, keepdims=True).astype(jnp.int32)
@@ -220,8 +208,8 @@
     slot = div(first + turn, devices)
     placing = one_hot(block * FOLD, jnp.where(turn < amount, piece * block + slot, -1))
 
-    tokens = lanes_of(tokens_in[...])
-    chosen = jnp.sum(jnp.where(best_hot, tokens, 0).astype(jnp.float32), axis=1, keepdims=True)
+    chosen = jnp.where(score == top, padded(tokens_in[...], 0), 0).astype(jnp.float32)
+    chosen = jnp.sum(chosen, axis=1, keepdims=True)
     chosen = chosen.astype(jnp.int32)
     for r in range(requests):
         length_ref[r] = length[r, 0]
@@ -236,8 +224,7 @@
     for part in range(FOLD):
         dest_ref[:, part * slab : (part + 1) * slab] = placed[part * block : (part + 1) * block, :]
 
-    arrived(near_counts, n_gx - 1, near_send)
-    arrived(counts, n_gy - 1, far_send)
+    arrived(counts, devices - 1, count_send)
     arrived(incoming, devices - 1, row_send)
 
 
@@ -278,12 +265,9 @@
                 pltpu.VMEM((devices, FOLD, slab), hidden.dtype),
                 pltpu.VMEM((devices, FOLD, slab), hidden.dtype),
                 pltpu.VMEM((1, 1, 128), jnp.int32),
-                pltpu.VMEM((n_gx, 1, 128), jnp.int32),
-                pltpu.VMEM((n_gy, n_gx, 1, 128), jnp.int32),
+                pltpu.VMEM((devices, 1, 128), jnp.int32),
                 pltpu.SemaphoreType.DMA,
                 pltpu.SemaphoreType.DMA((3,)),
-                pltpu.SemaphoreType.DMA,
-                pltpu.SemaphoreType.DMA,
                 pltpu.SemaphoreType.DMA,
                 pltpu.SemaphoreType.DMA,
                 pltpu.SemaphoreType.DMA,

time: 22.5 us -> 21.6 us (0.960)
  Pallas kernels: 21.7 us -> 20.7 us
    pallas_call x1, Pallas kernels: 21 us -> 20 us  [local(): pl.pallas_call(functools.partial(kernel, (n_gx, n_gy, requests, nodes, wi...]
where the time goes in v4:
time: 21.6 us; the launch traced here: 21.4 us
  Pallas kernels  20.7 us (96%)
  between operations  0.64 us (3%)
    pallas_call x1, Pallas kernels, local(): pl.pallas_call(functools.partial(kernel, (n_gx, n_gy, requests, nodes, wi...  20 us
    pallas_call x1, Pallas kernels, local(): pl.pallas_call(hand_on, out_shape=outs, in_specs=[anywhere] * len(outs),...  0.75 us

profile of v4, /device:TPU:0, one launch (start us, length us, event | category | flops | bytes accessed | tf_op | source)
XLA Modules:
  0.0 21.4 jit_solution(1710668491238766482)
XLA Ops:
  0.6 20.0 %shard_map.75 = (bf16[32,4096]{1,0:T(8,128)(2,1)S(1)}, s32[4]{0:T(128)S(1)}, s32[4]{0:T(128)S(1)}, s32[4]{0:T(128)S(1)}) custom-call(bf16[4,64,4096]{2,1,0:T(8,128)(2,1)} %hidden_ref.1, s32[4,64]{1,0:T(4,128)} %parents_ref.1, s32[4,64]{1,0:T(4,128)} %accepted_ref.1, s32[4,64]{1,0:T(4,128)} %tokens_ref.1), custom_call_target="tpu_custom_call" | custom-call | tf_op jit(solution)/shard_map/pallas_call | solution.py:254
  20.6 0.7 %shard_map.76 = (bf16[32,4096]{1,0:T(8,128)(2,1)}, s32[4]{0:T(128)}, s32[4]{0:T(128)}, s32[4]{0:T(128)}) custom-call(bf16[32,4096]{1,0:T(8,128)(2,1)S(1)} %get-tuple-element.8.refs_0_, s32[4]{0:T(128)S(1)} %get-tuple-element.9.refs_1_, s32[4]{0:T(128)S(1)} %get-tuple-element.10.refs_2_, s32[4]{0:T(128)S(1)} %get-tuple-element.11.refs_3_), custom_call_target="tpu_custom_call" | custom-call | tf_op jit(solution)/shard_map/pallas_call | solution.py:281

commit v5 on v4

--- a/solution.py
+++ b/solution.py
@@ -181,6 +181,13 @@
         turn = mod(peer + devices * block * devices - before, devices)
         outgoing[peer] = staged[jnp.minimum(turn, block)]
 
+    ring = n_gy // 2
+
+    def reach_of(step):
+        turn = step % n_gy // 2
+        return (-min(turn, ring - turn), -turn, -step)
+
+    far_first = sorted(range(1, devices), key=reach_of)
     row_copies = [
         pltpu.make_async_remote_copy(
             src_ref=outgoing.at[peer],
@@ -190,7 +197,7 @@
             device_id=place(peer),
             device_id_type=MESH,
         )
-        for peer in others(range(1, devices))
+        for peer in others(far_first)
     ]
     for copy in row_copies:
         copy.start()

time: 21.6 us -> 20.9 us (0.968)
  Pallas kernels: 20.7 us -> 20 us
    pallas_call x1, Pallas kernels: 20 us -> 19.3 us  [local(): pl.pallas_call(functools.partial(kernel, (n_gx, n_gy, requests, nodes, wi...]
where the time goes in v5:
time: 20.9 us; the launch traced here: 20.7 us
  Pallas kernels  20 us (96%)
  between operations  0.64 us (3%)
    pallas_call x1, Pallas kernels, local(): pl.pallas_call(functools.partial(kernel, (n_gx, n_gy, requests, nodes, wi...  19.3 us
    pallas_call x1, Pallas kernels, local(): pl.pallas_call(hand_on, out_shape=outs, in_specs=[anywhere] * len(outs),...  0.75 us

profile of v5, /device:TPU:0, one launch (start us, length us, event | category | flops | bytes accessed | tf_op | source)
XLA Modules:
  0.0 20.7 jit_solution(2543855614306454867)
XLA Ops:
  0.6 19.3 %shard_map.75 = (bf16[32,4096]{1,0:T(8,128)(2,1)S(1)}, s32[4]{0:T(128)S(1)}, s32[4]{0:T(128)S(1)}, s32[4]{0:T(128)S(1)}) custom-call(bf16[4,64,4096]{2,1,0:T(8,128)(2,1)} %hidden_ref.1, s32[4,64]{1,0:T(4,128)} %parents_ref.1, s32[4,64]{1,0:T(4,128)} %accepted_ref.1, s32[4,64]{1,0:T(4,128)} %tokens_ref.1), custom_call_target="tpu_custom_call" | custom-call | tf_op jit(solution)/shard_map/pallas_call | solution.py:261
  19.9 0.7 %shard_map.76 = (bf16[32,4096]{1,0:T(8,128)(2,1)}, s32[4]{0:T(128)}, s32[4]{0:T(128)}, s32[4]{0:T(128)}) custom-call(bf16[32,4096]{1,0:T(8,128)(2,1)S(1)} %get-tuple-element.8.refs_0_, s32[4]{0:T(128)S(1)} %get-tuple-element.9.refs_1_, s32[4]{0:T(128)S(1)} %get-tuple-element.10.refs_2_, s32[4]{0:T(128)S(1)} %get-tuple-element.11.refs_3_), custom_call_target="tpu_custom_call" | custom-call | tf_op jit(solution)/shard_map/pallas_call | solution.py:288
